TPU v7x, 32 devices: a whole 2x2x4 slice. The times are simulated.
32 devices in a mesh: fsdp: 8 (over z, x), side: 4 (over y, core).
Axes of the slice: x: 2, y: 2, z: 4, core: 2. Of those that a mesh axis runs over, the one named last changes fastest.
Arguments:
- attn_inputs: bfloat16 [4096, 5120], P(('side', 'fsdp')), may hold values from -6 to 6
- queries: bfloat16 [4096, 2560], P(('side', 'fsdp')), may hold values from -310 to 310
- key_vectors: bfloat16 [4096, 512], P(('side', 'fsdp')), may hold values from -12 to 12
- logp_grad: bfloat16 [4096, 2560], P(('side', 'fsdp')), may hold values from -24 to 24
- new_logp: float32 [4096], P(('side', 'fsdp')), may hold values from -6.5 to -0.01
- old_logp: float32 [4096], P(('side', 'fsdp')), may hold values from -4 to -0.05
- rewards: float32 [8], replicated, may hold values from -8 to 8
- group_ids: int32 [8], replicated, may hold values from 0 to 1
- lengths: int32 [8], replicated, may hold values from 256 to 512
- value_proj: bfloat16 [5120, 512], P('fsdp'), may hold values from -0.078125 to 0.078125
- first_moment: bfloat16 [5120, 512], P(('fsdp', 'side')), may hold values from -120 to 120
- second_moment: bfloat16 [5120, 512], P(('fsdp', 'side')), may hold values from 100 to 9984
Outputs:
- input_grad: bfloat16 [4096, 5120], P(('side', 'fsdp'))
- new_proj: bfloat16 [5120, 512], P('fsdp')
- new_first: bfloat16 [5120, 512], P(('fsdp', 'side'))
- new_second: bfloat16 [5120, 512], P(('fsdp', 'side'))
All inputs are finite; a program needn't handle non-finite values.
Results may differ from a plain program's by a relative error of at most 0.03.
Values may be sent and summed in bfloat16 or wider, within the bound.
No kernel may reach another device: no remote copies, remote signals or barrier semaphores. Data moves between devices by JAX's collectives and lax.ppermute only.
A program may use at most 64 MiB of HBM per device.

v0:
```python
import math
import jax
import jax.numpy as jnp
from jax import lax
from jax.sharding import PartitionSpec as P

QH = 20
KVH = 4
HEAD = 128
ROLLS = 2
clip_low = 0.8
clip_high = 1.2
decay_first = 0.9
decay_second = 0.95
step_rate = 0.001
weight_decay = 0.1
adam_eps = 1e-08
bias_first = 1.0 - 0.9**10
bias_second = 1.0 - 0.95**10


def advantages(rewards, group_ids):
    group_count = rewards.shape[0] // 4
    member = (group_ids[:, None] == jnp.arange(group_count, dtype=jnp.int32)[None, :]).astype(
        jnp.float32
    )
    counts = jnp.maximum(jnp.sum(member, axis=0), 1.0)
    group_mean = jnp.sum(member * rewards[:, None], axis=0) / counts
    own_mean = jnp.sum(member * group_mean[None, :], axis=1)
    spread = rewards - own_mean
    variance = jnp.sum(member * (spread * spread)[:, None], axis=0) / counts
    own_std = jnp.sqrt(jnp.sum(member * variance[None, :], axis=1))
    return spread / jnp.maximum(own_std, 1.0)


def coefficient(new_lp, old_lp, adv_tok, len_tok, pos_tok, full_len):
    ratio_now = jnp.exp(new_lp - old_lp)
    clipped = jnp.clip(ratio_now, clip_low, clip_high)
    active = (ratio_now * adv_tok <= clipped * adv_tok) & (pos_tok < len_tok)
    len_weight = full_len / len_tok.astype(jnp.float32)
    return jnp.where(active, -adv_tok * ratio_now * len_weight, 0.0)


def block_values(query_blk, grad_blk, roll_keys, first_pos):
    tok_rows = query_blk.shape[0]
    key_count = roll_keys.shape[0]
    per_group = QH // KVH
    score_scale = 1.0 / math.sqrt(HEAD)
    query_pos = first_pos + jnp.arange(tok_rows, dtype=jnp.int32)
    key_pos = jnp.arange(key_count, dtype=jnp.int32)
    allowed = jnp.tile(key_pos[None, :] <= query_pos[:, None], (per_group, 1))
    pieces = []
    for kv_head in range(KVH):
        col_low = kv_head * per_group * HEAD
        col_high = col_low + per_group * HEAD
        q_part = (
            query_blk[:, col_low:col_high]
            .reshape(tok_rows, per_group, HEAD)
            .transpose(1, 0, 2)
            .reshape(per_group * tok_rows, HEAD)
        )
        g_part = (
            grad_blk[:, col_low:col_high]
            .reshape(tok_rows, per_group, HEAD)
            .transpose(1, 0, 2)
            .reshape(per_group * tok_rows, HEAD)
        )
        k_part = roll_keys[:, kv_head * HEAD : (kv_head + 1) * HEAD]
        scores = jnp.dot(q_part, k_part.T, preferred_element_type=jnp.float32) * score_scale
        scores = jnp.where(allowed, scores, -1e30)
        top_val = jnp.max(scores, axis=1, keepdims=True)
        expo = jnp.exp(scores - top_val)
        attention = (expo / jnp.sum(expo, axis=1, keepdims=True)).astype(jnp.bfloat16)
        pieces.append(jnp.dot(attention.T, g_part, preferred_element_type=jnp.float32))
    return jnp.concatenate(pieces, axis=1)


def adam_rows(old_rows, grad_rows, first_moment, second_moment):
    first = decay_first * first_moment.astype(jnp.float32) + (1.0 - decay_first) * grad_rows
    second = (
        decay_second * second_moment.astype(jnp.float32)
        + (1.0 - decay_second) * grad_rows * grad_rows
    )
    weight_now = old_rows.astype(jnp.float32)
    update = (
        first / bias_first / (jnp.sqrt(second / bias_second) + adam_eps) + weight_decay * weight_now
    )
    return (
        (weight_now - step_rate * update).astype(jnp.bfloat16),
        first.astype(jnp.bfloat16),
        second.astype(jnp.bfloat16),
    )


def shards(
    attn_inputs,
    queries,
    key_vectors,
    logp_grad,
    new_logp,
    old_logp,
    rewards,
    group_ids,
    lengths,
    value_proj,
    first_moment,
    second_moment,
):
    fsdp_size = lax.axis_size("fsdp")
    fsdp_index = lax.axis_index("fsdp")
    side_index = lax.axis_index("side")
    tok_rows = attn_inputs.shape[0]
    half = tok_rows // ROLLS
    full_len = half * fsdp_size
    width = key_vectors.shape[1]
    first_pos = fsdp_index * half
    advantage = advantages(rewards, group_ids)
    slot = jnp.arange(tok_rows, dtype=jnp.int32)
    global_roll = side_index * ROLLS + slot // half
    position = first_pos + slot % half
    coeff = coefficient(
        new_logp, old_logp, advantage[global_roll], lengths[global_roll], position, full_len
    )
    out_grad = (coeff[:, None] * logp_grad.astype(jnp.float32)).astype(jnp.bfloat16)
    in_columns = lax.all_to_all(attn_inputs, "fsdp", split_axis=1, concat_axis=0, tiled=True)
    all_keys = lax.all_gather(key_vectors, "fsdp", axis=0, tiled=True)
    keys_split = all_keys.reshape(fsdp_size, ROLLS, half, width)
    partials = []
    for roll in range(ROLLS):
        roll_keys = keys_split[:, roll].reshape(full_len, width)
        partials.append(
            block_values(
                queries[roll * half : (roll + 1) * half],
                out_grad[roll * half : (roll + 1) * half],
                roll_keys,
                first_pos,
            )
        )
    stacked = jnp.stack(partials, axis=0)
    placed = (
        stacked.reshape(ROLLS, fsdp_size, half, width)
        .transpose(1, 0, 2, 3)
        .reshape(fsdp_size * tok_rows, width)
    )
    values_grad = lax.psum(placed.astype(jnp.bfloat16), "fsdp")
    grad_cols = jnp.dot(values_grad, value_proj.T, preferred_element_type=jnp.float32).astype(
        jnp.bfloat16
    )
    input_grad = lax.all_to_all(grad_cols, "fsdp", split_axis=0, concat_axis=1, tiled=True)
    weight_grad = lax.dot_general(
        in_columns, values_grad, (((0,), (0,)), ((), ())), preferred_element_type=jnp.float32
    )
    shard_grad = lax.psum_scatter(
        weight_grad.astype(jnp.bfloat16), "side", scatter_dimension=0, tiled=True
    ).astype(jnp.float32)
    shard_rows = shard_grad.shape[0]
    old_rows = lax.dynamic_slice_in_dim(value_proj, side_index * shard_rows, shard_rows, 0)
    new_rows, new_first, new_second = adam_rows(old_rows, shard_grad, first_moment, second_moment)
    new_proj = lax.all_gather(new_rows, "side", axis=0, tiled=True)
    return (input_grad, new_proj, new_first, new_second)


def solution(mesh):
    placed = (
        P(("side", "fsdp"), None),
        P(("side", "fsdp"), None),
        P(("side", "fsdp"), None),
        P(("side", "fsdp"), None),
        P(("side", "fsdp")),
        P(("side", "fsdp")),
        P(),
        P(),
        P(),
        P("fsdp", None),
        P(("fsdp", "side"), None),
        P(("fsdp", "side"), None),
    )
    return jax.shard_map(
        shards,
        mesh=mesh,
        in_specs=placed,
        out_specs=(
            P(("side", "fsdp"), None),
            P("fsdp", None),
            P(("fsdp", "side"), None),
            P(("fsdp", "side"), None),
        ),
        check_vma=False,
    )
```

profile of v0, /device:TPU:0, one launch (start us, length us, event | category | flops | bytes accessed | tf_op | source)
XLA Modules:
  0.0 208.1 jit_solution(15375847009809611103)
XLA Ops:
  7.2 0.7 all-gather.2.cloned.1.call-update
  7.9 2.4 %copy.153 = bf16[128,5120]{0,1:T(8,128)(2,1)} copy(bf16[128,5120]{1,0:T(8,128)(2,1)} %param.12) | data formatting | bytes 2621440 | tf_op args[0]
  10.4 7.4 %all-to-all-start.1 = ((bf16[128,8,640]{0,2,1:T(8,128)(2,1)}), bf16[128,8,640]{0,2,1:T(8,128)(2,1)S(1)}, u32[]{:S(2)}, u32[]{:S(2)}) async-start(bf16[128,8,640]{0,2,1:T(8,128)(2,1)} %bitcast.61), calls=%async_computation.1 | async-start | bytes 2621440 | tf_op jit(solution)/shard_map/all_to_all | solution.py:125
  18.4 0.7 fusion.40
  19.1 0.7 fusion.41
  19.7 10.1 %and_select_fusion = f32[128]{0:T(128)S(1)} fusion(f32[128]{0:T(128)S(1)} %copy-done.10, f32[128]{0:T(128)S(1)} %copy-done.11, s32[]{:T(128)} %bitcast.16, f32[]{:T(128)} %bitcast.7, s32[]{:T(128)} %bitcast.17, f32[]{:T(128)} %bitcast.8, s32[]{:T(128)} %bitcast.18, f32[]{:T(128)} %bitcast.9, s32[]{:T(128)} %bitcast.19, f32[]{:T(128)} %bitcast.10, ...), kind=kLoop, calls=%fused_computation.78 | loop fusion | flops 6784 | bytes 1608 | tf_op jit(solution)/shard_map/jit(_where)/select_n | solution.py:41
  30.3 0.7 copy-done.2
  32.9 0.6 copy.149
  33.8 28.8 %all-gather.2.cloned.1.call-done = bf16[1024,512]{1,0:T(8,128)(2,1)} async-done(((bf16[128,512]{1,0:T(8,128)(2,1)}), bf16[1024,512]{1,0:T(8,128)(2,1)}) %all-gather.2.cloned.1.call-update) | async-done | bytes 1048592 | tf_op jit(solution)/shard_map/all_gather | solution.py:126
  62.7 1.3 fusion.37
  67.2 0.4 convolution_convert_fusion.8
  67.8 0.4 convolution_convert_fusion.9
  68.5 0.4 convolution_convert_fusion.7
  69.1 0.4 convolution_convert_fusion.6
  69.8 0.4 convolution_convert_fusion.5
  70.4 0.4 convolution_convert_fusion.4
  71.1 1.0 copy.141
  72.4 0.4 convolution_convert_fusion.3
  72.7 0.5 copy-done.5
  73.9 0.8 copy-done
  74.8 1.1 copy.151
  75.9 77.6 %all-reduce.2.cloned.1.call-done = bf16[1024,512]{1,0:T(8,128)(2,1)} async-done(((bf16[1024,512]{1,0:T(8,128)(2,1)}), bf16[1024,512]{1,0:T(8,128)(2,1)}) %all-reduce.2.cloned.1.call-update) | async-done | bytes 1048592 | tf_op jit(solution)/shard_map/psum | solution.py:145
  153.5 3.3 %convolution_convert_fusion = bf16[1024,640]{1,0:T(8,128)(2,1)} fusion(bf16[1024,512]{1,0:T(8,128)(2,1)} %all-reduce.2.cloned.1.call-done, bf16[640,512]{1,0:T(8,128)(2,1)S(1)} %copy-done.6), kind=kOutput, calls=%fused_computation | convolution fusion | flops 671744000 | bytes 3014656 | tf_op jit(solution)/shard_map/dot_general | solution.py:146
  156.8 4.2 %all-to-all-start = ((bf16[8,128,640]{2,1,0:T(8,128)(2,1)}), bf16[8,128,640]{2,1,0:T(8,128)(2,1)S(1)}, u32[]{:S(2)}, u32[]{:S(2)}) async-start(bf16[8,128,640]{2,1,0:T(8,128)(2,1)} %bitcast.127), calls=%async_computation | async-start | bytes 2621440 | tf_op jit(solution)/shard_map/all_to_all | solution.py:149
  161.0 1.5 copy.154
  162.5 2.7 %fusion = bf16[640,512]{0,1:T(8,128)(2,1)S(1)} fusion(bf16[1024,512]{1,0:T(8,128)(2,1)} %all-reduce.2.cloned.1.call-done, bf16[1024,640]{1,0:T(8,128)(2,1)} %bitcast.129), kind=kOutput, calls=%fused_computation.3 | convolution fusion | flops 671416320 | bytes 3014656 | tf_op jit(solution)/shard_map/dot_general | solution.py:150
  165.2 1.1 copy.156
  166.3 23.9 %reduce-scatter.4.cloned.1.call-done = bf16[160,512]{1,0:T(8,128)(2,1)} async-done(((bf16[640,512]{1,0:T(8,128)(2,1)}), bf16[160,512]{1,0:T(8,128)(2,1)}) %reduce-scatter.4.cloned.1.call-update) | async-done | bytes 163856 | tf_op jit(solution)/shard_map/reduce_scatter | solution.py:153
  190.2 1.9 fusion.23
  192.2 7.3 %all_gather.7 = bf16[640,512]{1,0:T(8,128)(2,1)S(1)} all-gather(bf16[160,512]{1,0:T(8,128)(2,1)S(1)} %get-tuple-element.47), channel_id=1, replica_groups=mesh['fsdp'=8,'side'=4] {'side'}, dimensions={0}, use_global_device_ids=true | all-gather | bytes 819200 | tf_op jit(solution)/shard_map/all_gather | solution.py:159
  199.5 1.2 copy.158
  200.7 0.8 copy.169
  (94 shorter events, 8.9 us)
Async XLA Ops:
  7.2 55.5 %all-gather.2.cloned.1.call-start = ((), (), s32[]{:S(2)}) async-start(), calls=%async_computation.3 | async-start | bytes 1179648 | tf_op jit(solution)/shard_map/all_gather | solution.py:126
  10.3 7.5 %copy-start.8 = (f32[8]{0:T(128)S(1)}, f32[8]{0:T(128)}, u32[]{:S(2)}) copy-start(f32[8]{0:T(128)} %param.18) | copy-start | bytes 100
  10.3 7.5 %copy-start.9 = (s32[8]{0:T(128)S(1)}, s32[8]{0:T(128)}, u32[]{:S(2)}) copy-start(s32[8]{0:T(128)} %param.19) | copy-start | bytes 100
  10.3 8.7 %copy-start.7 = (s32[8]{0:T(128)S(1)}, s32[8]{0:T(128)}, u32[]{:S(2)}) copy-start(s32[8]{0:T(128)} %param.20) | copy-start | bytes 100
  10.3 9.4 %copy-start.10 = (f32[128]{0:T(128)S(1)}, f32[128]{0:T(128)}, u32[]{:S(2)}) copy-start(f32[128]{0:T(128)} %param.16) | copy-start | bytes 1540
  10.4 9.4 %copy-start.11 = (f32[128]{0:T(128)S(1)}, f32[128]{0:T(128)}, u32[]{:S(2)}) copy-start(f32[128]{0:T(128)} %param.17) | copy-start | bytes 1540
  10.4 19.5 %copy-start.1 = (bf16[128,2560]{1,0:T(8,128)(2,1)S(1)}, bf16[128,2560]{1,0:T(8,128)(2,1)}, u32[]{:S(2)}) copy-start(bf16[128,2560]{1,0:T(8,128)(2,1)} %param.15) | copy-start | bytes 1966084
  10.4 146.4 %all-to-all-start.1 = ((bf16[128,8,640]{0,2,1:T(8,128)(2,1)}), bf16[128,8,640]{0,2,1:T(8,128)(2,1)S(1)}, u32[]{:S(2)}, u32[]{:S(2)}) async-start(bf16[128,8,640]{0,2,1:T(8,128)(2,1)} %bitcast.61), calls=%async_computation.1 | async-start | bytes 2621440 | tf_op jit(solution)/shard_map/all_to_all | solution.py:125
  17.8 135.7 %all-reduce.2.cloned.1.call-start = ((), (), s32[]{:S(2)}) async-start(), calls=%async_computation.4 | async-start | bytes 2097152 | tf_op jit(solution)/shard_map/psum | solution.py:145
  29.8 1.1 copy-start.2
  72.4 0.9 copy-start.5
  73.6 1.0 copy-start
  74.8 78.7 %copy-start.6 = (bf16[640,512]{1,0:T(8,128)(2,1)S(1)}, bf16[640,512]{1,0:T(8,128)(2,1)}, u32[]{:S(2)}) copy-start(bf16[640,512]{1,0:T(8,128)(2,1)} %param.21) | copy-start | bytes 1966084
  156.8 42.7 %all-to-all-start = ((bf16[8,128,640]{2,1,0:T(8,128)(2,1)}), bf16[8,128,640]{2,1,0:T(8,128)(2,1)S(1)}, u32[]{:S(2)}, u32[]{:S(2)}) async-start(bf16[8,128,640]{2,1,0:T(8,128)(2,1)} %bitcast.127), calls=%async_computation | async-start | bytes 2621440 | tf_op jit(solution)/shard_map/all_to_all | solution.py:149
  161.0 29.2 %reduce-scatter.4.cloned.1.call-start = ((), (), s32[]{:S(2)}) async-start(), calls=%async_computation.5 | async-start | bytes 819200 | tf_op jit(solution)/shard_map/reduce_scatter | solution.py:153
  165.2 25.1 %copy-start.3 = (bf16[160,512]{1,0:T(8,128)(2,1)S(1)}, bf16[160,512]{1,0:T(8,128)(2,1)}, u32[]{:S(2)}) copy-start(bf16[160,512]{1,0:T(8,128)(2,1)} %param.23) | copy-start | bytes 491524
  165.2 25.1 %copy-start.4 = (bf16[160,512]{1,0:T(8,128)(2,1)S(1)}, bf16[160,512]{1,0:T(8,128)(2,1)}, u32[]{:S(2)}) copy-start(bf16[160,512]{1,0:T(8,128)(2,1)} %param.22) | copy-start | bytes 491524
Sparse Core Ops, SparseCore 0:
  10.1 52.5 all-gather.1
  76.0 77.4 all-reduce.1
  166.4 23.7 reduce-scatter.3
where the time goes:
time: 209 us; the launch traced here: 208 us
  waiting for transfers between devices  131 us (63%)
  local copies, waits for them, and re-layouts  16.8 us (8%)
  other arithmetic  15.1 us (7%)
  between operations  14.2 us (7%)
  matrix products  11.8 us (6%)
  starting transfers between devices  11.7 us (6%)
  blocking collectives  7.31 us (3%)
    psum x1, waiting for transfers between devices, shards(): values_grad = lax.psum(placed.astype(jnp.bfloat16), 'fsdp')  77.6 us
    all_gather x1, waiting for transfers between devices, shards(): all_keys = lax.all_gather(key_vectors, 'fsdp', axis=0, tiled=True)  28.8 us
    reduce_scatter x1, waiting for transfers between devices, shards(): lax.psum_scatter(weight_grad.astype(jnp.bfloat16), 'side', scatter_dimens...  23.9 us
    select_n x1, other arithmetic, coefficient(): return jnp.where(active, -adv_tok * ratio_now * len_weight, 0.0)  10.1 us
    all_to_all x1, starting transfers between devices, shards(): lax.all_to_all(attn_inputs, 'fsdp', split_axis=1, concat_axis=0, tiled=True)  7.42 us
    all_gather x1, blocking collectives, shards(): new_proj = lax.all_gather(new_rows, 'side', axis=0, tiled=True)  7.31 us
    unnamed x27, local copies, waits for them, and re-layouts  6.41 us
    all_to_all x1, starting transfers between devices, shards(): lax.all_to_all(grad_cols, 'fsdp', split_axis=0, concat_axis=1, tiled=True)  4.21 us
  transfers between devices with their start and end apart: 5, of which 3 were waited for; matrix products, arithmetic and copies ran while one was open for 19% of the time, Pallas kernels for 0%

commit v1 on v0

--- a/solution.py
+++ b/solution.py
@@ -123,7 +123,16 @@
     )
     out_grad = (coeff[:, None] * logp_grad.astype(jnp.float32)).astype(jnp.bfloat16)
     in_columns = lax.all_to_all(attn_inputs, "fsdp", split_axis=1, concat_axis=0, tiled=True)
-    all_keys = lax.all_gather(key_vectors, "fsdp", axis=0, tiled=True)
+    fan = lax.axis_size("fsdp")
+    heard = key_vectors
+    store = [heard]
+    f_next = [(j0 - 1, j0) for j0 in range(1, fan)] + [(fan - 1, 0)]
+    for _ in range(fan - 1):
+        heard = lax.ppermute(heard, axis_name="fsdp", perm=f_next)
+        store += [heard]
+    u1 = jnp.concatenate([*reversed(store)], axis=0)
+    long_array = lax.axis_index("fsdp")
+    all_keys = jnp.roll(u1, (long_array + 1) * heard.shape[0], axis=0)
     keys_split = all_keys.reshape(fsdp_size, ROLLS, half, width)
     partials = []
     for roll in range(ROLLS):

time: 209 us -> 233 us (1.11)
  waiting for transfers between devices: 131 us -> 143 us
  starting transfers between devices: 11.7 us -> 19.8 us
  local copies, waits for them, and re-layouts: 16.8 us -> 20.5 us
    ppermute x0 -> x7, waiting for transfers between devices: none -> 41.4 us  [shards(): heard = lax.ppermute(heard, axis_name='fsdp', perm=f_next)]
    all_gather x1 -> x0, waiting for transfers between devices: 28.8 us -> none  [shards(): all_keys = lax.all_gather(key_vectors, 'fsdp', axis=0, tiled=True)]
    ppermute x0 -> x7, starting transfers between devices: none -> 10.5 us  [shards(): heard = lax.ppermute(heard, axis_name='fsdp', perm=f_next)]
    transpose x8, local copies, waits for them, and re-layouts: 0.75 us -> 4.54 us  [block_values(): g_part = grad_blk[:, col_low:col_high].reshape(tok_rows, per_group, HEAD)...]
    all_to_all x1, starting transfers between devices: 7.42 us -> 5.01 us  [shards(): lax.all_to_all(attn_inputs, 'fsdp', split_axis=1, concat_axis=0, tiled=True)]
    unnamed x27 -> x58, local copies, waits for them, and re-layouts: 6.41 us -> 5.28 us
  transfers between devices with their start and end apart: 5 -> 11, of which waited for: 3 -> 6; matrix products, arithmetic and copies ran while one was open for 19% -> 19% of each run, Pallas kernels for 0% -> 0%
where the time goes in v1:
time: 233 us; the launch traced here: 232 us
  waiting for transfers between devices  143 us (61%)
  local copies, waits for them, and re-layouts  20.5 us (9%)
  starting transfers between devices  19.8 us (8%)
  other arithmetic  15.1 us (6%)
  between operations  14.6 us (6%)
  matrix products  11.8 us (5%)
  blocking collectives  7.29 us (3%)
    psum x1, waiting for transfers between devices, shards(): values_grad = lax.psum(placed.astype(jnp.bfloat16), 'fsdp')  77.5 us
    ppermute x7, waiting for transfers between devices, shards(): heard = lax.ppermute(heard, axis_name='fsdp', perm=f_next)  41.4 us
    reduce_scatter x1, waiting for transfers between devices, shards(): lax.psum_scatter(weight_grad.astype(jnp.bfloat16), 'side', scatter_dimens...  23.9 us
    ppermute x7, starting transfers between devices, shards(): heard = lax.ppermute(heard, axis_name='fsdp', perm=f_next)  10.5 us
    select_n x1, other arithmetic, coefficient(): return jnp.where(active, -adv_tok * ratio_now * len_weight, 0.0)  10.1 us
    all_gather x1, blocking collectives, shards(): new_proj = lax.all_gather(new_rows, 'side', axis=0, tiled=True)  7.29 us
    unnamed x58, local copies, waits for them, and re-layouts  5.28 us
    all_to_all x1, starting transfers between devices, shards(): lax.all_to_all(attn_inputs, 'fsdp', split_axis=1, concat_axis=0, tiled=True)  5.01 us
  transfers between devices with their start and end apart: 11, of which 6 were waited for; matrix products, arithmetic and copies ran while one was open for 19% of the time, Pallas kernels for 0%

profile of v1, /device:TPU:0, one launch (start us, length us, event | category | flops | bytes accessed | tf_op | source)
XLA Modules:
  0.0 232.0 jit_solution(806722511974436444)
XLA Ops:
  7.2 3.0 %collective-permute-start = (bf16[128,512]{1,0:T(8,128)(2,1)}, bf16[128,512]{1,0:T(8,128)(2,1)S(1)}, u32[]{:S(2)}, u32[]{:S(2)}) collective-permute-start(bf16[128,512]{1,0:T(8,128)(2,1)} %param.14), channel_id=1, source_target_pairs={{0,4},{4,8},{8,12},{12,16},{16,20},{20,24},{24,28},{28,0},{1,5},{5... | collective-permute-start | bytes 393224 | tf_op jit(solution)/shard_map/ppermute | solution.py:131
  10.2 2.4 %copy.153 = bf16[128,5120]{0,1:T(8,128)(2,1)} copy(bf16[128,5120]{1,0:T(8,128)(2,1)} %param.12) | data formatting | bytes 2621440 | tf_op args[0]
  12.7 5.0 %all-to-all-start.1 = ((bf16[128,8,640]{0,2,1:T(8,128)(2,1)}), bf16[128,8,640]{0,2,1:T(8,128)(2,1)S(1)}, u32[]{:S(2)}, u32[]{:S(2)}) async-start(bf16[128,8,640]{0,2,1:T(8,128)(2,1)} %bitcast.69), calls=%async_computation.1 | async-start | bytes 2621440 | tf_op jit(solution)/shard_map/all_to_all | solution.py:125
  18.3 2.0 collective-permute-start.1
  20.3 0.7 fusion.48
  21.0 0.7 fusion.49
  21.6 24.8 %collective-permute-done.1 = bf16[128,512]{1,0:T(8,128)(2,1)S(1)} collective-permute-done((bf16[128,512]{1,0:T(8,128)(2,1)S(1)}, bf16[128,512]{1,0:T(8,128)(2,1)S(1)}, u32[]{:S(2)}, u32[]{:S(2)}) %collective-permute-start.1) | collective-permute-done | bytes 131104 | tf_op jit(solution)/shard_map/ppermute | solution.py:131
  46.4 10.1 %and_select_fusion = f32[128]{0:T(128)S(1)} fusion(f32[128]{0:T(128)S(1)} %copy-done.18, f32[128]{0:T(128)S(1)} %copy-done.19, s32[]{:T(128)} %bitcast.17, f32[]{:T(128)} %bitcast.8, s32[]{:T(128)} %bitcast.18, f32[]{:T(128)} %bitcast.9, s32[]{:T(128)} %bitcast.19, f32[]{:T(128)} %bitcast.10, s32[]{:T(128)} %bitcast.20, f32[]{:T(128)} %bitcast.11, ...), kind=kLoop, calls=%fused_computation.102 | loop fusion | flops 6784 | bytes 1608 | tf_op jit(solution)/shard_map/jit(_where)/select_n | solution.py:41
  57.0 7.3 %collective-permute-done.3 = bf16[128,512]{1,0:T(8,128)(2,1)S(1)} collective-permute-done((bf16[128,512]{1,0:T(8,128)(2,1)S(1)}, bf16[128,512]{1,0:T(8,128)(2,1)S(1)}, u32[]{:S(2)}, u32[]{:S(2)}) %collective-permute-start.3) | collective-permute-done | bytes 131104 | tf_op jit(solution)/shard_map/ppermute | solution.py:131
  64.2 1.8 collective-permute-start.4
  66.0 0.7 fusion.46
  66.7 5.1 %collective-permute-done.4 = bf16[128,512]{1,0:T(8,128)(2,1)S(1)} collective-permute-done((bf16[128,512]{1,0:T(8,128)(2,1)S(1)}, bf16[128,512]{1,0:T(8,128)(2,1)S(1)}, u32[]{:S(2)}, u32[]{:S(2)}) %collective-permute-start.4) | collective-permute-done | bytes 131104 | tf_op jit(solution)/shard_map/ppermute | solution.py:131
  71.9 0.7 fusion.47
  72.8 1.0 reshape.227
  76.5 0.6 copy.140
  77.4 0.6 copy.143
  78.3 0.6 copy.145
  80.1 3.3 %collective-permute-start.6 = (bf16[128,512]{1,0:T(8,128)(2,1)S(1)}, bf16[128,512]{1,0:T(8,128)(2,1)S(1)}, u32[]{:S(2)}, u32[]{:S(2)}) collective-permute-start(bf16[128,512]{1,0:T(8,128)(2,1)S(1)} %collective-permute-done.5), channel_id=1, source_target_pairs={{0,4},{4,8},{8,12},{12,16},{16,20},{20,24},{24,28},{28,0},{1,5},{5... | collective-permute-start | bytes 393224 | tf_op jit(solution)/shard_map/ppermute | solution.py:131
  83.6 4.2 %collective-permute-done.6 = bf16[128,512]{1,0:T(8,128)(2,1)S(1)} collective-permute-done((bf16[128,512]{1,0:T(8,128)(2,1)S(1)}, bf16[128,512]{1,0:T(8,128)(2,1)S(1)}, u32[]{:S(2)}, u32[]{:S(2)}) %collective-permute-start.6) | collective-permute-done | bytes 131104 | tf_op jit(solution)/shard_map/ppermute | solution.py:131
  95.5 1.0 copy.141
  98.5 1.1 copy.151
  99.6 77.5 %all-reduce.2.cloned.1.call-done = bf16[1024,512]{1,0:T(8,128)(2,1)} async-done(((bf16[1024,512]{1,0:T(8,128)(2,1)}), bf16[1024,512]{1,0:T(8,128)(2,1)}) %all-reduce.2.cloned.1.call-update) | async-done | bytes 1048592 | tf_op jit(solution)/shard_map/psum | solution.py:154
  177.1 3.3 %convolution_convert_fusion = bf16[1024,640]{1,0:T(8,128)(2,1)} fusion(bf16[1024,512]{1,0:T(8,128)(2,1)} %all-reduce.2.cloned.1.call-done, bf16[640,512]{1,0:T(8,128)(2,1)S(1)} %copy-done.14), kind=kOutput, calls=%fused_computation | convolution fusion | flops 671744000 | bytes 3014656 | tf_op jit(solution)/shard_map/dot_general | solution.py:155
  180.4 4.2 %all-to-all-start = ((bf16[8,128,640]{2,1,0:T(8,128)(2,1)}), bf16[8,128,640]{2,1,0:T(8,128)(2,1)S(1)}, u32[]{:S(2)}, u32[]{:S(2)}) async-start(bf16[8,128,640]{2,1,0:T(8,128)(2,1)} %bitcast.160), calls=%async_computation | async-start | bytes 2621440 | tf_op jit(solution)/shard_map/all_to_all | solution.py:158
  184.6 1.5 copy.154
  186.1 2.7 %fusion = bf16[640,512]{0,1:T(8,128)(2,1)S(1)} fusion(bf16[1024,512]{1,0:T(8,128)(2,1)} %all-reduce.2.cloned.1.call-done, bf16[1024,640]{1,0:T(8,128)(2,1)} %bitcast.162), kind=kOutput, calls=%fused_computation.3 | convolution fusion | flops 671416320 | bytes 3014656 | tf_op jit(solution)/shard_map/dot_general | solution.py:159
  188.8 1.1 copy.156
  189.9 23.9 %reduce-scatter.4.cloned.1.call-done = bf16[160,512]{1,0:T(8,128)(2,1)} async-done(((bf16[640,512]{1,0:T(8,128)(2,1)}), bf16[160,512]{1,0:T(8,128)(2,1)}) %reduce-scatter.4.cloned.1.call-update) | async-done | bytes 163856 | tf_op jit(solution)/shard_map/reduce_scatter | solution.py:162
  213.9 1.9 fusion.31
  215.8 7.3 %all_gather.3 = bf16[640,512]{1,0:T(8,128)(2,1)S(1)} all-gather(bf16[160,512]{1,0:T(8,128)(2,1)S(1)} %get-tuple-element.47), channel_id=1, replica_groups=mesh['fsdp'=8,'side'=4] {'side'}, dimensions={0}, use_global_device_ids=true | all-gather | bytes 819200 | tf_op jit(solution)/shard_map/all_gather | solution.py:168
  223.1 1.2 copy.158
  224.3 0.8 copy.184
  (138 shorter events, 15.0 us)
Async XLA Ops:
  7.2 10.6 %copy-start.16 = (f32[8]{0:T(128)S(1)}, f32[8]{0:T(128)}, u32[]{:S(2)}) copy-start(f32[8]{0:T(128)} %param.18) | copy-start | bytes 100
  7.2 10.6 %copy-start.17 = (s32[8]{0:T(128)S(1)}, s32[8]{0:T(128)}, u32[]{:S(2)}) copy-start(s32[8]{0:T(128)} %param.19) | copy-start | bytes 100
  7.2 13.8 %copy-start.15 = (s32[8]{0:T(128)S(1)}, s32[8]{0:T(128)}, u32[]{:S(2)}) copy-start(s32[8]{0:T(128)} %param.20) | copy-start | bytes 100
  7.2 39.2 %copy-start.18 = (f32[128]{0:T(128)S(1)}, f32[128]{0:T(128)}, u32[]{:S(2)}) copy-start(f32[128]{0:T(128)} %param.16) | copy-start | bytes 1540
  7.2 39.2 %copy-start.19 = (f32[128]{0:T(128)S(1)}, f32[128]{0:T(128)}, u32[]{:S(2)}) copy-start(f32[128]{0:T(128)} %param.17) | copy-start | bytes 1540
  7.2 49.6 %copy-start.1 = (bf16[128,2560]{1,0:T(8,128)(2,1)S(1)}, bf16[128,2560]{1,0:T(8,128)(2,1)}, u32[]{:S(2)}) copy-start(bf16[128,2560]{1,0:T(8,128)(2,1)} %param.15) | copy-start | bytes 1966084
  7.2 11.0 %collective-permute-start = (bf16[128,512]{1,0:T(8,128)(2,1)}, bf16[128,512]{1,0:T(8,128)(2,1)S(1)}, u32[]{:S(2)}, u32[]{:S(2)}) collective-permute-start(bf16[128,512]{1,0:T(8,128)(2,1)} %param.14), channel_id=1, source_target_pairs={{0,4},{4,8},{8,12},{12,16},{16,20},{20,24},{24,28},{28,0},{1,5},{5... | collective-permute-start | bytes 393224 | tf_op jit(solution)/shard_map/ppermute | solution.py:131
  12.7 53.4 %copy-start.2 = (bf16[128,2560]{1,0:T(8,128)(2,1)S(1)}, bf16[128,2560]{1,0:T(8,128)(2,1)}, u32[]{:S(2)}) copy-start(bf16[128,2560]{1,0:T(8,128)(2,1)} %param.13) | copy-start | bytes 1966084
  12.7 167.7 %all-to-all-start.1 = ((bf16[128,8,640]{0,2,1:T(8,128)(2,1)}), bf16[128,8,640]{0,2,1:T(8,128)(2,1)S(1)}, u32[]{:S(2)}, u32[]{:S(2)}) async-start(bf16[128,8,640]{0,2,1:T(8,128)(2,1)} %bitcast.69), calls=%async_computation.1 | async-start | bytes 2621440 | tf_op jit(solution)/shard_map/all_to_all | solution.py:125
  17.7 159.4 %all-reduce.2.cloned.1.call-start = ((), (), s32[]{:S(2)}) async-start(), calls=%async_computation.3 | async-start | bytes 2097152 | tf_op jit(solution)/shard_map/psum | solution.py:154
  18.3 28.1 %collective-permute-start.1 = (bf16[128,512]{1,0:T(8,128)(2,1)S(1)}, bf16[128,512]{1,0:T(8,128)(2,1)S(1)}, u32[]{:S(2)}, u32[]{:S(2)}) collective-permute-start(bf16[128,512]{1,0:T(8,128)(2,1)S(1)} %collective-permute-done), channel_id=1, source_target_pairs={{0,4},{4,8},{8,12},{12,16},{16,20},{20,24},{24,28},{28,0},{1,5},{5... | collective-permute-start | bytes 393224 | tf_op jit(solution)/shard_map/ppermute | solution.py:131
  46.4 10.1 %collective-permute-start.2 = (bf16[128,512]{1,0:T(8,128)(2,1)S(1)}, bf16[128,512]{1,0:T(8,128)(2,1)S(1)}, u32[]{:S(2)}, u32[]{:S(2)}) collective-permute-start(bf16[128,512]{1,0:T(8,128)(2,1)S(1)} %collective-permute-done.1), channel_id=1, source_target_pairs={{0,4},{4,8},{8,12},{12,16},{16,20},{20,24},{24,28},{28,0},{1,5},{5... | collective-permute-start | bytes 393224 | tf_op jit(solution)/shard_map/ppermute | solution.py:131
  56.5 7.7 %collective-permute-start.3 = (bf16[128,512]{1,0:T(8,128)(2,1)S(1)}, bf16[128,512]{1,0:T(8,128)(2,1)S(1)}, u32[]{:S(2)}, u32[]{:S(2)}) collective-permute-start(bf16[128,512]{1,0:T(8,128)(2,1)S(1)} %collective-permute-done.2), channel_id=1, source_target_pairs={{0,4},{4,8},{8,12},{12,16},{16,20},{20,24},{24,28},{28,0},{1,5},{5... | collective-permute-start | bytes 393224 | tf_op jit(solution)/shard_map/ppermute | solution.py:131
  64.2 7.7 %collective-permute-start.4 = (bf16[128,512]{1,0:T(8,128)(2,1)S(1)}, bf16[128,512]{1,0:T(8,128)(2,1)S(1)}, u32[]{:S(2)}, u32[]{:S(2)}) collective-permute-start(bf16[128,512]{1,0:T(8,128)(2,1)S(1)} %collective-permute-done.3), channel_id=1, source_target_pairs={{0,4},{4,8},{8,12},{12,16},{16,20},{20,24},{24,28},{28,0},{1,5},{5... | collective-permute-start | bytes 393224 | tf_op jit(solution)/shard_map/ppermute | solution.py:131
  66.7 7.7 %copy-start.4 = (bf16[64,640]{1,0:T(8,128)(2,1)S(1)}, bf16[64,640]{1,0:T(8,128)(2,1)}, u32[]{:S(2)}) copy-start(bf16[64,640]{1,0:T(8,128)(2,1)} %get-tuple-element.35) | copy-start | bytes 245764
  71.9 8.2 %collective-permute-start.5 = (bf16[128,512]{1,0:T(8,128)(2,1)S(1)}, bf16[128,512]{1,0:T(8,128)(2,1)S(1)}, u32[]{:S(2)}, u32[]{:S(2)}) collective-permute-start(bf16[128,512]{1,0:T(8,128)(2,1)S(1)} %collective-permute-done.4), channel_id=1, source_target_pairs={{0,4},{4,8},{8,12},{12,16},{16,20},{20,24},{24,28},{28,0},{1,5},{5... | collective-permute-start | bytes 393224 | tf_op jit(solution)/shard_map/ppermute | solution.py:131
  78.1 9.8 %copy-start.3 = (bf16[128,512]{1,0:T(8,128)(2,1)S(1)}, bf16[128,512]{1,0:T(8,128)(2,1)}, u32[]{:S(2)}) copy-start(bf16[128,512]{1,0:T(8,128)(2,1)} %param.14) | copy-start | bytes 393220
  80.1 7.7 %collective-permute-start.6 = (bf16[128,512]{1,0:T(8,128)(2,1)S(1)}, bf16[128,512]{1,0:T(8,128)(2,1)S(1)}, u32[]{:S(2)}, u32[]{:S(2)}) collective-permute-start(bf16[128,512]{1,0:T(8,128)(2,1)S(1)} %collective-permute-done.5), channel_id=1, source_target_pairs={{0,4},{4,8},{8,12},{12,16},{16,20},{20,24},{24,28},{28,0},{1,5},{5... | collective-permute-start | bytes 393224 | tf_op jit(solution)/shard_map/ppermute | solution.py:131
  90.1 1.4 copy-start.7
  91.2 0.9 copy-start.8
  91.9 0.9 copy-start.9
  92.5 0.9 copy-start.11
  93.2 0.9 copy-start.12
  93.8 0.9 copy-start.13
  96.5 0.9 copy-start.10
  97.3 1.0 copy-start
  98.5 78.6 %copy-start.14 = (bf16[640,512]{1,0:T(8,128)(2,1)S(1)}, bf16[640,512]{1,0:T(8,128)(2,1)}, u32[]{:S(2)}) copy-start(bf16[640,512]{1,0:T(8,128)(2,1)} %param.21) | copy-start | bytes 1966084
  180.4 42.7 %all-to-all-start = ((bf16[8,128,640]{2,1,0:T(8,128)(2,1)}), bf16[8,128,640]{2,1,0:T(8,128)(2,1)S(1)}, u32[]{:S(2)}, u32[]{:S(2)}) async-start(bf16[8,128,640]{2,1,0:T(8,128)(2,1)} %bitcast.160), calls=%async_computation | async-start | bytes 2621440 | tf_op jit(solution)/shard_map/all_to_all | solution.py:158
  184.6 29.3 %reduce-scatter.4.cloned.1.call-start = ((), (), s32[]{:S(2)}) async-start(), calls=%async_computation.4 | async-start | bytes 819200 | tf_op jit(solution)/shard_map/reduce_scatter | solution.py:162
  186.1 27.8 %copy-start.5 = (bf16[160,512]{1,0:T(8,128)(2,1)S(1)}, bf16[160,512]{1,0:T(8,128)(2,1)}, u32[]{:S(2)}) copy-start(bf16[160,512]{1,0:T(8,128)(2,1)} %param.23) | copy-start | bytes 491524
  186.1 27.8 %copy-start.6 = (bf16[160,512]{1,0:T(8,128)(2,1)S(1)}, bf16[160,512]{1,0:T(8,128)(2,1)}, u32[]{:S(2)}) copy-start(bf16[160,512]{1,0:T(8,128)(2,1)} %param.22) | copy-start | bytes 491524
Sparse Core Ops, SparseCore 0:
  99.7 77.3 all-reduce.1
  190.0 23.7 reduce-scatter.3
